TPU v7x, 32 devices: a whole 2x2x4 slice. The times are simulated.
32 devices in a mesh: groups: 2 (over x), ctx: 8 (over z, y), head: 2 (over core).
Axes of the slice: x: 2, y: 2, z: 4, core: 2. Of those that a mesh axis runs over, the one named last changes fastest.
Arguments:
- query_nope: bfloat16 [32, 128, 128], P('groups', ('ctx', 'head')), parts along dimension 0, may hold values from -6 to 6
- query_rope: bfloat16 [32, 8192], P('groups', ('ctx', 'head')), parts along dimension 0, may hold values from -31 to 31
- key_absorb: bfloat16 [128, 128, 512], P(('ctx', 'head')), may hold values from -0.5 to 0.5
- value_absorb: bfloat16 [128, 512, 128], P(('ctx', 'head')), may hold values from -4 to 4
- output_weight: bfloat16 [16384, 7168], P(('ctx', 'head')), may hold values from -0.0625 to 0.0625
- latent_cache: bfloat16 [3584, 64, 576], P(('groups', 'ctx')), parts along dimension 0, may hold values from -4 to 4
- page_owner: int32 [3584], P(('groups', 'ctx')), parts along dimension 0, may hold values from -1 to 15, as said below
Outputs:
- layer_output: bfloat16 [32, 7168], P('groups', ('ctx', 'head')), parts along dimension 0
There are 2 independent parts, one for each index of `groups`. A program takes and returns all parts, laid end to end along the dimension named above; an argument that names none is the same for every part. Nothing has to cross between parts.
Inputs may be any that keep to these rules, and one draw needn't show every extreme that they name: `page_owner`: a slot's request, or -1 for an unused slot; every request owns at least one slot; every index of ctx has an eighth of its 224 slots or more in use, and some index has all 224 in use.
All inputs are finite; a program needn't handle non-finite values.
Results may differ from a plain program's by a relative error of at most 0.03.
Values may be sent and summed in bfloat16 or wider, within the bound.
A program may use at most 128 MiB of HBM per device.

v0:
```python
import functools

import jax
import jax.numpy as jnp
from jax import lax
from jax.experimental import pallas as pl
from jax.experimental.pallas import tpu as pltpu
from jax.sharding import PartitionSpec as P

PARTS = 2
F32 = jnp.float32
BF16 = jnp.bfloat16


def dot_nt(a, b):
    return lax.dot_general(a, b, (((1,), (1,)), ((), ())), preferred_element_type=F32)


def attention_kernel(heads_here, group, score_scale, owner_hbm, q_ref, cache_ref, sum_ref, stat_ref,
                     owner_ref, owner_sem, pages, query, scores, peak, total, acc, sems):
    ctx = q_ref.shape[0]
    slots, heads, _ = acc.shape
    requests = slots - 1
    page_count, page_len, _ = pages.shape
    latent = acc.shape[2]
    chunks = sems.shape[0]
    chunk = page_count // chunks

    def fetch(i):
        window = pl.ds(i * chunk, chunk)
        return pltpu.make_async_copy(cache_ref.at[window], pages.at[window], sems.at[i])

    owner_load = pltpu.make_async_copy(owner_hbm, owner_ref, owner_sem)
    owner_load.start()
    for i in range(chunks):
        fetch(i).start()
    for r in range(requests):
        rows = [q_ref[c, r * heads_here:(r + 1) * heads_here, :].astype(F32) for c in range(ctx)]
        query[r] = jnp.concatenate(rows, axis=0).astype(BF16)
    peak[...] = jnp.full_like(peak, -1e30)
    total[...] = jnp.zeros_like(total)
    acc[...] = jnp.zeros_like(acc)
    owner_load.wait()

    def owner_of(page):
        owner = owner_ref[page]
        return jnp.where(owner < 0, requests, owner)

    def score_group(base):
        owners = [owner_of(base + j) for j in range(group)]
        for j in range(group):
            found = dot_nt(query[jnp.minimum(owners[j], requests - 1)], pages[base + j]) * score_scale
            scores[base + j] = found
            peak[owners[j]] = jnp.maximum(peak[owners[j]], found)

    @pl.loop(0, chunks)
    def _(i):
        fetch(i).wait()

        @pl.loop(0, chunk // group)
        def _(g):
            score_group(i * chunk + g * group)

    for r in range(slots):
        peak[r] = jnp.broadcast_to(jnp.max(peak[r], axis=1, keepdims=True), peak.shape[1:])

    @pl.loop(0, page_count // group)
    def _(g):
        base = g * group
        owners = [owner_of(base + j) for j in range(group)]
        weights = []
        for j in range(group):
            weight = jnp.exp(scores[base + j] - peak[owners[j]])
            total[owners[j]] = total[owners[j]] + weight
            weights.append(weight.astype(BF16))
        for j in range(group):
            acc[owners[j]] = acc[owners[j]] + jnp.dot(
                weights[j], pages[base + j, :, :latent], preferred_element_type=F32)

    lane = lax.broadcasted_iota(jnp.int32, (heads, stat_ref.shape[-1]), 1)
    top = jnp.zeros(lane.shape, F32)
    norm = jnp.zeros(lane.shape, F32)
    for r in range(requests):
        top = jnp.where(lane == r, jnp.max(peak[r], axis=1, keepdims=True), top)
        norm = jnp.where(lane == r, jnp.sum(total[r], axis=1, keepdims=True), norm)
    for c in range(ctx):
        rows = slice(c * heads_here, (c + 1) * heads_here)
        part = acc[:requests, rows, :]
        sum_ref[c % 2, c // 2] = part.reshape(requests * heads_here, latent).astype(BF16)
        stat_ref[c % 2, c // 2, 0] = top[rows]
        stat_ref[c % 2, c // 2, 1] = norm[rows]


def attention(gathered, cache, owners, requests, heads_here, latent, score_scale):
    ctx, _, entry = gathered.shape
    page_count, page_len, _ = cache.shape
    heads = ctx * heads_here
    sum_shape = (2, ctx // 2, requests * heads_here, latent)
    stat_shape = (2, ctx // 2, 2, heads_here, 128)
    chunks = next(n for n in (14, 8, 7, 4, 2, 1) if page_count % n == 0)
    group = next(n for n in (16, 8, 4, 2, 1) if (page_count // chunks) % n == 0)
    return pl.pallas_call(
        functools.partial(attention_kernel, heads_here, group, score_scale),
        in_specs=[
            pl.BlockSpec(memory_space=pltpu.HBM),
            pl.BlockSpec(memory_space=pltpu.VMEM),
            pl.BlockSpec(memory_space=pltpu.HBM),
        ],
        out_specs=[pl.BlockSpec(memory_space=pltpu.VMEM)] * 2,
        scratch_shapes=[
            pltpu.SMEM((page_count,), jnp.int32),
            pltpu.SemaphoreType.DMA,
            pltpu.VMEM((page_count, page_len, entry), BF16),
            pltpu.VMEM((requests, heads, entry), BF16),
            pltpu.VMEM((page_count, heads, page_len), F32),
            pltpu.VMEM((requests + 1, heads, page_len), F32),
            pltpu.VMEM((requests + 1, heads, page_len), F32),
            pltpu.VMEM((requests + 1, heads, latent), F32),
            pltpu.SemaphoreType.DMA((chunks,)),
        ],
        out_shape=[
            jax.ShapeDtypeStruct(sum_shape, BF16),
            jax.ShapeDtypeStruct(stat_shape, F32),
        ],
        compiler_params=pltpu.CompilerParams(vmem_limit_bytes=48 << 20),
    )(owners, gathered, cache)


def remote(src, dst, send_sem, recv_sem, where):
    return pltpu.make_async_remote_copy(
        src_ref=src, dst_ref=dst, send_sem=send_sem, recv_sem=recv_sem,
        device_id=where, device_id_type=pl.DeviceIdType.MESH)


def gather_kernel(nz, nope_hbm, rope_hbm, key_hbm, out_ref, nope_ref, rope_ref, key_ref, in_sems, wide, rows, mine,
                  y_send, y_recv, up_send, up_recv, down_send, down_recv):
    requests, heads_here, _ = nope_ref.shape
    latent = key_ref.shape[2]
    rope = rope_ref.shape[1] // heads_here
    me = lax.axis_index("ctx")
    z, y = me // 2, me % 2
    partner = {"ctx": z * 2 + 1 - y}
    above, below = {"ctx": me + 2}, {"ctx": me - 2}
    has_above, has_below = z + 1 < nz, z > 0
    loads = [
        pltpu.make_async_copy(src, dst, in_sems.at[i])
        for i, (src, dst) in enumerate(((nope_hbm, nope_ref), (rope_hbm, rope_ref), (key_hbm, key_ref)))
    ]
    for load in loads:
        load.start()

    barrier = pltpu.get_barrier_semaphore()
    pl.semaphore_signal(barrier, inc=1, device_id=partner, device_id_type=pl.DeviceIdType.MESH)

    @pl.when(has_above)
    def _():
        pl.semaphore_signal(barrier, inc=1, device_id=above, device_id_type=pl.DeviceIdType.MESH)

    @pl.when(has_below)
    def _():
        pl.semaphore_signal(barrier, inc=1, device_id=below, device_id_type=pl.DeviceIdType.MESH)

    for load in loads:
        load.wait()
    wide[...] = nope_ref[...].astype(F32)
    for h in range(heads_here):
        rows[:, h, :latent] = jnp.dot(wide[:, h, :].astype(BF16), key_ref[h], preferred_element_type=F32)
        rows[:, h, latent:] = rope_ref[:, h * rope:(h + 1) * rope].astype(F32)
    value = rows[...].reshape(requests * heads_here, latent + rope).astype(BF16)
    mine[...] = value
    out_ref[me] = value

    pl.semaphore_wait(barrier, 1 + has_above.astype(jnp.int32) + has_below.astype(jnp.int32))

    depth = mine.shape[0] // PARTS

    def block(ref, part):
        return ref.at[part * depth:(part + 1) * depth]

    def across(origin, part, src=None):
        slot, i = block(out_ref.at[origin * 2 + y], part), origin * PARTS + part
        return remote(slot if src is None else block(src, part), slot, y_send.at[i], y_recv.at[i], partner)

    def upward(step, part, src=None):
        slot, i = block(out_ref.at[me - 2 * step], part), step * PARTS + part
        return remote(slot if src is None else block(src, part), slot, up_send.at[i], up_recv.at[i], above)

    def downward(step, part, src=None):
        slot, i = block(out_ref.at[me + 2 * step], part), step * PARTS + part
        return remote(slot if src is None else block(src, part), slot, down_send.at[i], down_recv.at[i], below)

    def arrival(row, part, sem):
        slot = block(out_ref.at[row], part)
        return remote(slot, slot, sem, sem, partner)

    for part in range(PARTS):
        @pl.when(has_above)
        def _():
            upward(0, part, mine).start()

        @pl.when(has_below)
        def _():
            downward(0, part, mine).start()

        across(z, part, mine).start()
    for step in range(nz - 1):
        for part in range(PARTS):
            @pl.when(z - 1 - step >= 0)
            def _():
                arrival(me - 2 * (step + 1), part, up_recv.at[step * PARTS + part]).wait_recv()
                if step + 1 < nz - 1:
                    @pl.when(has_above)
                    def _():
                        upward(step + 1, part).start()
                across(z - 1 - step, part).start()

            @pl.when(z + 1 + step < nz)
            def _():
                arrival(me + 2 * (step + 1), part, down_recv.at[step * PARTS + part]).wait_recv()
                if step + 1 < nz - 1:
                    @pl.when(has_below)
                    def _():
                        downward(step + 1, part).start()
                across(z + 1 + step, part).start()

    for part in range(PARTS):
        for origin in range(nz):
            across(origin, part, mine).wait_send()
            arrival(origin * 2 + 1 - y, part, y_recv.at[origin * PARTS + part]).wait_recv()
        for step in range(nz - 1):
            @pl.when(has_above & (z - step >= 0))
            def _():
                upward(step, part, mine).wait_send()

            @pl.when(has_below & (z + step < nz))
            def _():
                downward(step, part, mine).wait_send()


def gather_queries(query_nope, query_rope, key_absorb, ctx):
    requests, heads_here, nope = query_nope.shape
    entry = key_absorb.shape[2] + query_rope.shape[1] // heads_here
    nz = ctx // 2
    vmem = pl.BlockSpec(memory_space=pltpu.VMEM)
    dma = pltpu.SemaphoreType.DMA
    return pl.pallas_call(
        functools.partial(gather_kernel, nz),
        out_shape=jax.ShapeDtypeStruct((ctx, requests * heads_here, entry), BF16),
        in_specs=[pl.BlockSpec(memory_space=pltpu.HBM)] * 3,
        out_specs=vmem,
        scratch_shapes=[
            pltpu.VMEM(query_nope.shape, BF16),
            pltpu.VMEM(query_rope.shape, BF16),
            pltpu.VMEM(key_absorb.shape, BF16),
            dma((3,)),
            pltpu.VMEM(query_nope.shape, F32),
            pltpu.VMEM((requests, heads_here, entry), F32),
            pltpu.VMEM((requests * heads_here, entry), BF16),
            dma((nz * PARTS,)), dma((nz * PARTS,)), dma((nz * PARTS,)),
            dma((nz * PARTS,)), dma((nz * PARTS,)), dma((nz * PARTS,)),
        ],
        compiler_params=pltpu.CompilerParams(collective_id=0, has_side_effects=True, vmem_limit_bytes=16 << 20),
    )(query_nope, query_rope, key_absorb)


def project_kernel(ctx, sum_ref, stat_ref, value_hbm, weight_ref, out_ref,
                   weight, value_ref, value_sem, y_sum, y_stat, c_sum, c_stat, z_sum, z_stat, wide,
                   h_keep, h_out, h_in, p_out, p_in,
                   w_sem, ys_send, ys_recv, yt_send, yt_recv, zs_send, zs_recv, zt_send, zt_recv,
                   h_send, h_recv, p_send, p_recv):
    nz = ctx // 2
    requests, half = out_ref.shape
    block = 2 * half
    heads_here, latent, _ = value_ref.shape
    me, core = lax.axis_index("ctx"), lax.axis_index("head")
    z, y = me // 2, me % 2
    partner, twin = {"ctx": z * 2 + 1 - y}, {"head": 1 - core}

    barrier = pltpu.get_barrier_semaphore()
    for k in range(1, ctx):
        pl.semaphore_signal(barrier, inc=1, device_id={"ctx": (me + k) % ctx}, device_id_type=pl.DeviceIdType.MESH)
    pl.semaphore_signal(barrier, inc=1, device_id=twin, device_id_type=pl.DeviceIdType.MESH)
    load = pltpu.make_async_copy(weight_ref, weight, w_sem)
    value_load = pltpu.make_async_copy(value_hbm, value_ref, value_sem)
    value_load.start()
    load.start()
    pl.semaphore_wait(barrier, ctx)

    depth = y_sum.shape[1] // PARTS

    def lines(part):
        return slice(part * depth, (part + 1) * depth)

    stat_copy = remote(stat_ref.at[1 - y], y_stat, yt_send, yt_recv, partner)
    stat_copy.start()
    y_copies = []
    for k in range(nz):
        target = (z + 1 + k) % nz
        for part in range(PARTS):
            i = k * PARTS + part
            copy = remote(sum_ref.at[1 - y, target, lines(part)], y_sum.at[k, lines(part)],
                          ys_send.at[i], ys_recv.at[i], partner)
            copy.start()
            y_copies.append(copy)
    stat_copy.wait_recv()

    def spread(factor):
        return jnp.concatenate([factor[:, r:r + 1] for r in range(requests)], axis=0)

    z_copies, z_stats = [], []
    for k in range(nz):
        target = (z + 1 + k) % nz
        top_a, norm_a = stat_ref[y, target, 0], stat_ref[y, target, 1]
        top_b, norm_b = y_stat[target, 0], y_stat[target, 1]
        top = jnp.maximum(top_a, top_b)
        keep_a, keep_b = jnp.exp(top_a - top), jnp.exp(top_b - top)
        norm = keep_a * norm_a + keep_b * norm_b
        rows_a, rows_b = spread(keep_a), spread(keep_b)
        there = {"ctx": target * 2 + y}
        if k < nz - 1:
            c_stat[k, 0] = top
            c_stat[k, 1] = norm
            copy = remote(c_stat.at[k], z_stat.at[k], zt_send.at[k], zt_recv.at[k], there)
            copy.start()
            z_stats.append(copy)
        both = []
        for part in range(PARTS):
            i = k * PARTS + part
            y_copies[i].wait_recv()
            both.append(rows_a[lines(part)] * sum_ref[y, target, lines(part)].astype(F32)
                        + rows_b[lines(part)] * y_sum[k, lines(part)].astype(F32))
            if k < nz - 1:
                c_sum[k, lines(part)] = both[part].astype(BF16)
                copy = remote(c_sum.at[k, lines(part)], z_sum.at[k, lines(part)], zs_send.at[i], zs_recv.at[i], there)
                copy.start()
                z_copies.append(copy)
    both = jnp.concatenate(both, axis=0)
    for copy in z_stats:
        copy.wait_recv()
    highest = top
    for k in range(nz - 1):
        highest = jnp.maximum(highest, z_stat[k, 0])
    keep = jnp.exp(top - highest)
    all_norm = keep * norm
    factors = []
    for k in range(nz - 1):
        factors.append(jnp.exp(z_stat[k, 0] - highest))
        all_norm = all_norm + factors[k] * z_stat[k, 1]
    safe = jnp.where(all_norm > 0, all_norm, 1.0)
    total = spread(keep / safe) * both
    for k in range(nz - 1):
        for part in range(PARTS):
            z_copies[k * PARTS + part].wait_recv()
        total = total + spread(factors[k] / safe) * z_sum[k].astype(F32)
    wide[...] = total.reshape(requests, heads_here, latent)
    outs = []
    value_load.wait()
    for h in range(heads_here):
        outs.append(jnp.dot(wide[:, h, :].astype(BF16), value_ref[h], preferred_element_type=F32).astype(BF16))
    head_out = jnp.concatenate(outs, axis=1)
    load.wait()

    aligned = block % 128 == 0
    h_copies, p_copies = [], []

    def place(k):
        return (me + 1 + k) % ctx if aligned else k

    def forward(k):
        target = place(k)
        h_copies[k].wait_recv()
        merged = h_keep[k] + h_in[k]
        if aligned:
            p_out[k] = merged.astype(BF16)
            if k < ctx - 1:
                copy = remote(p_out.at[k], p_in.at[k], p_send.at[k], p_recv.at[k], {"ctx": target})
                copy.start()
                p_copies.append(copy)
        else:
            p_out[k] = merged.astype(BF16)

            @pl.when(target != me)
            def _():
                slot = (target - me + ctx - 1) % ctx
                remote(p_out.at[k], p_in.at[slot], p_send.at[slot], p_recv.at[slot], {"ctx": target}).start()

    for k in range(ctx):
        if aligned:
            columns = weight[:, pl.ds(pl.multiple_of(place(k) * block, 128), block)]
        else:
            columns = weight[:, k * block:(k + 1) * block]
        part = jnp.dot(head_out, columns, preferred_element_type=F32)
        low, high = part[:, :half], part[:, half:]
        h_keep[k] = jnp.where(core == 0, low, high)
        h_out[k] = jnp.where(core == 0, high, low)
        copy = remote(h_out.at[k], h_in.at[k], h_send.at[k], h_recv.at[k], twin)
        copy.start()
        h_copies.append(copy)
        if k > 0:
            forward(k - 1)
    forward(ctx - 1)
    if aligned:
        result = h_keep[ctx - 1] + h_in[ctx - 1]
    else:
        result = p_out[me].astype(F32)
    for k in range(ctx - 1):
        remote(p_out.at[k], p_in.at[k], p_send.at[k], p_recv.at[k], partner).wait_recv()
        result = result + p_in[k].astype(F32)
    out_ref[...] = result.astype(BF16)
    for k in range(ctx - 1):
        remote(p_out.at[k], p_in.at[k], p_send.at[k], p_recv.at[k], partner).wait_send()
    for copy in h_copies + z_copies + z_stats + y_copies + [stat_copy]:
        copy.wait_send()


def project(sums, stats, value_absorb, output_weight, ctx):
    nz = ctx // 2
    _, _, rows, latent = sums.shape
    heads_here = value_absorb.shape[0]
    requests = rows // heads_here
    half = output_weight.shape[1] // (2 * ctx)
    vmem = pl.BlockSpec(memory_space=pltpu.VMEM)
    dma = pltpu.SemaphoreType.DMA
    stat_tail = stats.shape[2:]
    return pl.pallas_call(
        functools.partial(project_kernel, ctx),
        out_shape=jax.ShapeDtypeStruct((requests, half), BF16),
        in_specs=[vmem, vmem] + [pl.BlockSpec(memory_space=pltpu.HBM)] * 2,
        out_specs=vmem,
        scratch_shapes=[
            pltpu.VMEM(output_weight.shape, BF16),
            pltpu.VMEM(value_absorb.shape, BF16),
            dma,
            pltpu.VMEM((nz, rows, latent), BF16),
            pltpu.VMEM((nz,) + stat_tail, F32),
            pltpu.VMEM((nz - 1, rows, latent), BF16),
            pltpu.VMEM((nz - 1,) + stat_tail, F32),
            pltpu.VMEM((nz - 1, rows, latent), BF16),
            pltpu.VMEM((nz - 1,) + stat_tail, F32),
            pltpu.VMEM((requests, heads_here, latent), F32),
            pltpu.VMEM((ctx, requests, half), F32),
            pltpu.VMEM((ctx, requests, half), F32),
            pltpu.VMEM((ctx, requests, half), F32),
            pltpu.VMEM((ctx, requests, half), BF16),
            pltpu.VMEM((ctx - 1, requests, half), BF16),
            dma, dma((nz * PARTS,)), dma((nz * PARTS,)), dma, dma,
            dma(((nz - 1) * PARTS,)), dma(((nz - 1) * PARTS,)), dma((nz - 1,)), dma((nz - 1,)),
            dma((ctx,)), dma((ctx,)), dma((ctx - 1,)), dma((ctx - 1,)),
        ],
        compiler_params=pltpu.CompilerParams(collective_id=1, has_side_effects=True, vmem_limit_bytes=40 << 20),
    )(sums, stats, value_absorb, output_weight)


def body(ctx, query_nope, query_rope, key_absorb, value_absorb, output_weight, latent_cache, page_owner):
    requests, heads_here, nope_size = query_nope.shape
    latent_size = key_absorb.shape[2]
    rope_size = query_rope.shape[1] // heads_here
    score_scale = (nope_size + rope_size) ** (-0.5)
    query_nope, query_rope, key_absorb, page_owner = (
        pltpu.with_memory_space_constraint(x, pltpu.HBM) for x in (query_nope, query_rope, key_absorb, page_owner))
    gathered = gather_queries(query_nope, query_rope, key_absorb, ctx)
    sums, stats = attention(gathered, latent_cache, page_owner, requests, heads_here, latent_size, score_scale)
    return project(sums, stats, value_absorb, output_weight, ctx)


def solution(mesh):
    return jax.shard_map(
        functools.partial(body, mesh.shape["ctx"]),
        mesh=mesh,
        in_specs=(
            P("groups", ("ctx", "head"), None),
            P("groups", ("ctx", "head")),
            P(("ctx", "head"), None, None),
            P(("ctx", "head"), None, None),
            P(("ctx", "head"), None),
            P(("groups", "ctx"), None, None),
            P(("groups", "ctx")),
        ),
        out_specs=P("groups", ("ctx", "head")),
        check_vma=False,
    )
```

profile of v0, /device:TPU:0, one launch (start us, length us, event | category | flops | bytes accessed | tf_op | source)
XLA Modules:
  0.0 64.5 jit_solution(12186403345884318316)
XLA Ops:
  0.0 0.0 copy-start
  0.0 21.6 %shard_map.73.q_ref = bf16[8,128,576]{2,1,0:T(8,128)(2,1)S(1)} custom-call(bf16[16,8,128]{2,1,0:T(8,128)(2,1)} %nope_hbm.1, bf16[16,512]{1,0:T(8,128)(2,1)} %rope_hbm.1, bf16[8,128,512]{2,1,0:T(8,128)(2,1)} %key_hbm.1), custom_call_target="tpu_custom_call" | custom-call | tf_op jit(solution)/shard_map/pallas_call | solution.py:246
  21.6 16.0 %shard_map.74 = (bf16[2,4,128,512]{3,2,1,0:T(8,128)(2,1)S(1)}, f32[2,4,2,8,128]{4,3,2,1,0:T(8,128)S(1)}) custom-call(s32[224]{0:T(256)} %owner_hbm.1, bf16[8,128,576]{2,1,0:T(8,128)(2,1)S(1)} %shard_map.73.q_ref, bf16[224,64,576]{2,1,0:T(8,128)(2,1)} %cache_ref.1), custom_call_target="tpu_custom_call" | custom-call | tf_op jit(solution)/shard_map/pallas_call | solution.py:102
  37.6 0.0 copy-done
  37.6 26.3 %shard_map.75 = bf16[16,448]{1,0:T(8,128)(2,1)S(1)} custom-call(bf16[2,4,128,512]{3,2,1,0:T(8,128)(2,1)S(1)} %get-tuple-element.7.sum_ref, f32[2,4,2,8,128]{4,3,2,1,0:T(8,128)S(1)} %get-tuple-element.8.stat_ref, bf16[8,512,128]{2,1,0:T(8,128)(2,1)S(1)} %copy-done, bf16[1024,7168]{1,0:T(8,128)(2,1)} %weight_ref.1), custom_call_target="tpu_custom_call" | custom-call | tf_op jit(solution)/shard_map/pallas_call | solution.py:425
  63.9 0.6 copy.9
Async XLA Ops:
  0.0 37.6 %copy-start = (bf16[8,512,128]{2,1,0:T(8,128)(2,1)S(1)}, bf16[8,512,128]{2,1,0:T(8,128)(2,1)}, u32[]{:S(2)}) copy-start(bf16[8,512,128]{2,1,0:T(8,128)(2,1)} %value_hbm.1) | copy-start | bytes 3145732
where the time goes:
time: 64.7 us; the launch traced here: 64.5 us
  Pallas kernels  63.9 us (99%)
    pallas_call x1, Pallas kernels, project(): pl.pallas_call(functools.partial(project_kernel, ctx), out_shape=jax.Shap...  26.3 us
    pallas_call x1, Pallas kernels, gather_queries(): pl.pallas_call(functools.partial(gather_kernel, nz), out_shape=jax.ShapeD...  21.6 us
    pallas_call x1, Pallas kernels, attention(): pl.pallas_call(functools.partial(attention_kernel, heads_here, group, sco...  16 us

commit v1 on v0

v1 whole, which is shorter than its diff:
```python
import functools

import jax
import jax.numpy as jnp
from jax import lax
from jax.experimental import pallas as pl
from jax.experimental.pallas import tpu as pltpu
from jax.sharding import PartitionSpec as P

PARTS = 2
GROUP = 4
F32 = jnp.float32
BF16 = jnp.bfloat16
I32 = jnp.int32
LOW = -1e30


def dot_nt(a, b):
    return lax.dot_general(a, b, (((1,), (1,)), ((), ())), preferred_element_type=F32)


def remote(src, dst, send_sem, recv_sem, where):
    return pltpu.make_async_remote_copy(
        src_ref=src, dst_ref=dst, send_sem=send_sem, recv_sem=recv_sem,
        device_id=where, device_id_type=pl.DeviceIdType.MESH)


def up_to(n, step):
    return -(-n // step) * step


def column(row):
    n = row.shape[1]
    diagonal = lax.broadcasted_iota(I32, (n, n), 0) == lax.broadcasted_iota(I32, (n, n), 1)
    return jnp.sum(jnp.where(diagonal, jnp.broadcast_to(row, (n, n)), 0), axis=1, keepdims=True)


def plan_items(owner, requests, group, table, bias):
    count = owner.shape[1]
    width = up_to(count, 128)
    lanes_out = table.shape[1]
    items, tokens = bias.shape
    page = tokens // group
    owner = jnp.where(owner < 0, requests, owner)
    if width > count:
        owner = jnp.concatenate([owner, jnp.full((1, width - count), requests, I32)], axis=1)
    lane = lax.broadcasted_iota(I32, (1, width), 1)
    slot = lax.broadcasted_iota(I32, (width, 1), 0)
    lanes = lax.broadcasted_iota(I32, (width, width), 1)
    places = lax.broadcasted_iota(I32, (width, width), 0)
    key = owner * width + lane
    rank = jnp.sum(jnp.where(jnp.broadcast_to(key, (width, width)) < column(key), 1, 0), axis=1, keepdims=True)
    owner_c = column(owner)
    here = rank == lanes
    order = jnp.sum(jnp.where(here, slot, 0), axis=0, keepdims=True)
    sorted_owner = jnp.sum(jnp.where(here, owner_c, 0), axis=0, keepdims=True)
    before = jnp.sum(jnp.where(rank + 1 == lanes, owner_c, 0), axis=0, keepdims=True)
    opens = (lax.rem(lane, jnp.full(lane.shape, group, I32)) == 0) | (sorted_owner != before)
    start = column(jnp.where(opens & (sorted_owner < requests), 1, 0))
    order_c, sorted_c = column(order), column(sorted_owner)
    item = column(jnp.sum(jnp.where(places <= lanes, start, 0), axis=0, keepdims=True) - 1)
    place = lax.broadcasted_iota(I32, (width, lanes_out), 0)
    mine = (item == lax.broadcasted_iota(I32, (width, lanes_out), 1)) & (start > 0)

    def pick(value):
        return jnp.sum(jnp.where(mine, value, 0), axis=0, keepdims=True)

    first, who, real = pick(slot), pick(sorted_c), pick(start)
    first = first - lax.rem(first, jnp.full(first.shape, group, I32))
    tag = jnp.where(real > 0, who, -1)
    tag_c = column(tag)
    table[0:1, :] = who
    for j in range(group):
        chosen = place == first + j
        table[1 + j:2 + j, :] = jnp.sum(jnp.where(chosen, order_c, 0), axis=0, keepdims=True)
        theirs = column(jnp.sum(jnp.where(chosen, sorted_c, 0), axis=0, keepdims=True))
        fits = jnp.where(theirs[:items] == tag_c[:items], 0.0, LOW)
        bias[:, j * page:(j + 1) * page] = jnp.broadcast_to(fits, (items, page))
    index = lax.broadcasted_iota(I32, (1, lanes_out), 1)
    previous = jnp.where(index == 0, -1, pltpu.roll(tag, 1, 1))
    table[group + 1:group + 2, :] = jnp.where(tag == previous, 1, 0)
    owned = tag_c == lax.broadcasted_iota(I32, (lanes_out, lanes_out), 1)
    number = lax.broadcasted_iota(I32, (lanes_out, lanes_out), 0)
    table[group + 2:group + 3, :] = jnp.max(jnp.where(owned, number, 0), axis=0, keepdims=True)
    table[group + 3:group + 4, :] = jnp.max(jnp.where(owned, 1, 0), axis=0, keepdims=True)


def kernel(ctx, unroll, score_scale, nope_hbm, rope_hbm, key_hbm, owner_hbm, cache_hbm, value_hbm, weight_hbm, out_ref,
           nope_ref, rope_ref, key_ref, value_ref, weight, pages, in_sems, wide, rows_a, rows_b, mine_a, mine_b,
           all_a, all_b, y_send, y_recv, up_send, up_recv, down_send, down_recv,
           owner_ref, table, tab, bias, query_a, query_b, scores, marks, top_full, acc,
           sums, stats, y_sum, y_stat, c_sum, c_stat, z_sum, z_stat, attended,
           h_keep, h_out, h_in, p_out, p_in,
           ys_send, ys_recv, yt_send, yt_recv, zs_send, zs_recv, zt_send, zt_recv,
           h_send, h_recv, p_send, p_recv):
    requests, heads_here, _ = nope_ref.shape
    latent = key_ref.shape[2]
    cut = query_b.shape[2]
    rope = rope_ref.shape[1] // heads_here
    items = scores.shape[0]
    nz = ctx // 2
    half = out_ref.shape[1]
    block = 2 * half
    me, core = lax.axis_index("ctx"), lax.axis_index("head")
    z, y = me // 2, me % 2
    partner, twin = {"ctx": z * 2 + 1 - y}, {"head": 1 - core}
    above, below = {"ctx": me + 2}, {"ctx": me - 2}
    has_above, has_below = z + 1 < nz, z > 0

    def load(i, src, dst):
        return pltpu.make_async_copy(src, dst, in_sems.at[i])

    first_loads = [load(0, nope_hbm, nope_ref), load(1, rope_hbm, rope_ref), load(2, key_hbm, key_ref)]
    owner_load = load(3, owner_hbm, owner_ref)
    cache_load, value_load, weight_load = (
        load(4, cache_hbm, pages), load(5, value_hbm, value_ref), load(6, weight_hbm, weight))
    table_load = load(7, table, tab)
    for copy in first_loads:
        copy.start()
    owner_load.start()

    barrier = pltpu.get_barrier_semaphore()
    for k in range(1, ctx):
        pl.semaphore_signal(barrier, inc=1, device_id={"ctx": (me + k) % ctx}, device_id_type=pl.DeviceIdType.MESH)
    pl.semaphore_signal(barrier, inc=1, device_id=twin, device_id_type=pl.DeviceIdType.MESH)

    for copy in first_loads:
        copy.wait()
    cache_load.start()
    wide[...] = nope_ref[...].astype(F32)
    depth = mine_a.shape[0] // PARTS
    gathered = (all_a, all_b)

    def lines(part):
        return slice(part * depth, (part + 1) * depth)

    def block_of(which, row, part):
        return gathered[which].at[row, lines(part)]

    def sem(which, step, part):
        return (which * nz + step) * PARTS + part

    def across(which, origin, part, src=None):
        slot, i = block_of(which, origin * 2 + y, part), sem(which, origin, part)
        return remote(slot if src is None else src.at[lines(part)], slot, y_send.at[i], y_recv.at[i], partner)

    def upward(which, step, part, src=None):
        slot, i = block_of(which, me - 2 * step, part), sem(which, step, part)
        return remote(slot if src is None else src.at[lines(part)], slot, up_send.at[i], up_recv.at[i], above)

    def downward(which, step, part, src=None):
        slot, i = block_of(which, me + 2 * step, part), sem(which, step, part)
        return remote(slot if src is None else src.at[lines(part)], slot, down_send.at[i], down_recv.at[i], below)

    def arrival(which, row, part, done):
        slot = block_of(which, row, part)
        return remote(slot, slot, done, done, partner)

    mine = (mine_a, mine_b)

    def send_own(which):
        for part in range(PARTS):
            @pl.when(has_above)
            def _():
                upward(which, 0, part, mine[which]).start()

            @pl.when(has_below)
            def _():
                downward(which, 0, part, mine[which]).start()

            across(which, z, part, mine[which]).start()

    for h in range(heads_here):
        flat = wide[:, h, :].astype(BF16)
        rows_a[:, h, :cut] = jnp.dot(flat, key_ref[h, :, :cut], preferred_element_type=F32)
        rows_a[:, h, cut:] = rope_ref[:, h * rope:(h + 1) * rope].astype(F32)
    value = rows_a[...].reshape(requests * heads_here, cut + rope).astype(BF16)
    mine_a[...] = value
    all_a[me] = value
    pl.semaphore_wait(barrier, ctx)
    send_own(0)
    for h in range(heads_here):
        rows_b[:, h, :] = jnp.dot(wide[:, h, :].astype(BF16), key_ref[h, :, cut:], preferred_element_type=F32)
    value = rows_b[...].reshape(requests * heads_here, latent - cut).astype(BF16)
    mine_b[...] = value
    all_b[me] = value
    send_own(1)
    value_load.start()
    weight_load.start()

    owner_load.wait()
    plan_items(owner_ref[...], requests, GROUP, table, bias)
    table_load.start()

    def pass_on(which, step):
        for part in range(PARTS):
            @pl.when(z - 1 - step >= 0)
            def _():
                arrival(which, me - 2 * (step + 1), part, up_recv.at[sem(which, step, part)]).wait_recv()
                if step + 1 < nz - 1:
                    @pl.when(has_above)
                    def _():
                        upward(which, step + 1, part).start()
                across(which, z - 1 - step, part).start()

            @pl.when(z + 1 + step < nz)
            def _():
                arrival(which, me + 2 * (step + 1), part, down_recv.at[sem(which, step, part)]).wait_recv()
                if step + 1 < nz - 1:
                    @pl.when(has_below)
                    def _():
                        downward(which, step + 1, part).start()
                across(which, z + 1 + step, part).start()

    for step in range(nz - 1):
        pass_on(0, step)
        if step >= 1:
            pass_on(1, step - 1)
    pass_on(1, nz - 2)

    def settle(which, query):
        for origin in range(nz):
            for part in range(PARTS):
                arrival(which, origin * 2 + 1 - y, part, y_recv.at[sem(which, origin, part)]).wait_recv()
        for r in range(requests):
            lots = [gathered[which][c, r * heads_here:(r + 1) * heads_here, :].astype(F32) for c in range(ctx)]
            query[r] = jnp.concatenate(lots, axis=0).astype(BF16)

    settle(0, query_a)
    table_load.wait()
    cache_load.wait()

    def entries(i, columns):
        return jnp.concatenate([pages[tab[1 + j, i], :, columns] for j in range(GROUP)], axis=0)

    def first_scores(s, carry):
        for u in range(unroll):
            i = s * unroll + u
            asked = query_a.at[tab[0, i]]
            scores[i] = (dot_nt(asked[:, :cut], entries(i, slice(0, cut)))
                         + dot_nt(asked[:, cut:], entries(i, slice(latent, latent + rope))))
        return carry

    lax.fori_loop(0, items // unroll, first_scores, 0)
    settle(1, query_b)

    def last_scores(s, top):
        for u in range(unroll):
            i = s * unroll + u
            found = scores[i] + dot_nt(query_b[tab[0, i]], entries(i, slice(cut, latent)))
            found = found * score_scale + bias[pl.ds(i, 1), :]
            scores[i] = found
            top = jnp.where(tab[GROUP + 1, i] > 0, top, LOW)
            for j in range(found.shape[1] // 128):
                top = jnp.maximum(top, found[:, j * 128:(j + 1) * 128])
            marks[i] = top
        return top

    lax.fori_loop(0, items // unroll, last_scores, jnp.full(marks.shape[1:], LOW, F32))
    for r in range(requests):
        seen = marks[tab[GROUP + 2, r]]
        top_full[r] = jnp.broadcast_to(jnp.max(seen, axis=1, keepdims=True), seen.shape)

    def weigh(s, carry):
        total, held = carry
        for u in range(unroll):
            i = s * unroll + u
            keep = tab[GROUP + 1, i] > 0
            top = top_full[tab[0, i]]
            total = jnp.where(keep, total, 0.0)
            weights = []
            for j in range(scores.shape[2] // 128):
                weight_j = jnp.exp(scores[i, :, j * 128:(j + 1) * 128] - top)
                total = total + weight_j
                weights.append(weight_j.astype(BF16))
            marks[i] = total
            held = jnp.where(keep, held, 0.0) + jnp.dot(
                jnp.concatenate(weights, axis=1), entries(i, slice(0, latent)), preferred_element_type=F32)
            acc[i] = held
        return total, held

    lax.fori_loop(0, items // unroll, weigh, (jnp.zeros(marks.shape[1:], F32), jnp.zeros(acc.shape[1:], F32)))

    lane = lax.broadcasted_iota(I32, marks.shape[1:], 1)
    top = jnp.full(lane.shape, LOW, F32)
    norm = jnp.zeros(lane.shape, F32)
    for r in range(requests):
        here = (lane == r) & jnp.broadcast_to(tab[GROUP + 3, r] > 0, lane.shape)
        top = jnp.where(here, top_full[r], top)
        norm = jnp.where(here, jnp.sum(marks[tab[GROUP + 2, r]], axis=1, keepdims=True), norm)
    for c in range(ctx):
        rows = slice(c * heads_here, (c + 1) * heads_here)
        stats[c % 2, c // 2, 0] = top[rows]
        stats[c % 2, c // 2, 1] = norm[rows]
        lots = [acc[tab[GROUP + 2, r], rows, :] for r in range(requests)]
        sums[c % 2, c // 2] = jnp.concatenate(lots, axis=0).astype(BF16)

    stat_copy = remote(stats.at[1 - y], y_stat, yt_send, yt_recv, partner)
    stat_copy.start()
    y_copies = []
    for k in range(nz):
        target = (z + 1 + k) % nz
        for part in range(PARTS):
            i = k * PARTS + part
            copy = remote(sums.at[1 - y, target, lines(part)], y_sum.at[k, lines(part)],
                          ys_send.at[i], ys_recv.at[i], partner)
            copy.start()
            y_copies.append(copy)
    stat_copy.wait_recv()

    def spread(factor):
        return jnp.concatenate([factor[:, r:r + 1] for r in range(requests)], axis=0)

    z_copies, z_stats = [], []
    for k in range(nz):
        target = (z + 1 + k) % nz
        top_a, norm_a = stats[y, target, 0], stats[y, target, 1]
        top_b, norm_b = y_stat[target, 0], y_stat[target, 1]
        top = jnp.maximum(top_a, top_b)
        keep_a, keep_b = jnp.exp(top_a - top), jnp.exp(top_b - top)
        norm = keep_a * norm_a + keep_b * norm_b
        rows_x, rows_y = spread(keep_a), spread(keep_b)
        there = {"ctx": target * 2 + y}
        if k < nz - 1:
            c_stat[k, 0] = top
            c_stat[k, 1] = norm
            copy = remote(c_stat.at[k], z_stat.at[k], zt_send.at[k], zt_recv.at[k], there)
            copy.start()
            z_stats.append(copy)
        both = []
        for part in range(PARTS):
            i = k * PARTS + part
            y_copies[i].wait_recv()
            both.append(rows_x[lines(part)] * sums[y, target, lines(part)].astype(F32)
                        + rows_y[lines(part)] * y_sum[k, lines(part)].astype(F32))
            if k < nz - 1:
                c_sum[k, lines(part)] = both[part].astype(BF16)
                copy = remote(c_sum.at[k, lines(part)], z_sum.at[k, lines(part)], zs_send.at[i], zs_recv.at[i], there)
                copy.start()
                z_copies.append(copy)
    both = jnp.concatenate(both, axis=0)
    for copy in z_stats:
        copy.wait_recv()
    highest = top
    for k in range(nz - 1):
        highest = jnp.maximum(highest, z_stat[k, 0])
    keep = jnp.exp(top - highest)
    all_norm = keep * norm
    factors = []
    for k in range(nz - 1):
        factors.append(jnp.exp(z_stat[k, 0] - highest))
        all_norm = all_norm + factors[k] * z_stat[k, 1]
    safe = jnp.where(all_norm > 0, all_norm, 1.0)
    total = spread(keep / safe) * both
    for k in range(nz - 1):
        for part in range(PARTS):
            z_copies[k * PARTS + part].wait_recv()
        total = total + spread(factors[k] / safe) * z_sum[k].astype(F32)
    attended[...] = total.reshape(requests, heads_here, latent)
    outs = []
    value_load.wait()
    for h in range(heads_here):
        outs.append(jnp.dot(attended[:, h, :].astype(BF16), value_ref[h], preferred_element_type=F32).astype(BF16))
    head_out = jnp.concatenate(outs, axis=1)
    weight_load.wait()

    aligned = block % 128 == 0
    h_copies, p_copies = [], []

    def place(k):
        return (me + 1 + k) % ctx if aligned else k

    def forward(k):
        target = place(k)
        h_copies[k].wait_recv()
        merged = h_keep[k] + h_in[k]
        p_out[k] = merged.astype(BF16)
        if aligned:
            if k < ctx - 1:
                copy = remote(p_out.at[k], p_in.at[k], p_send.at[k], p_recv.at[k], {"ctx": target})
                copy.start()
                p_copies.append(copy)
        else:
            @pl.when(target != me)
            def _():
                slot = (target - me + ctx - 1) % ctx
                remote(p_out.at[k], p_in.at[slot], p_send.at[slot], p_recv.at[slot], {"ctx": target}).start()

    for k in range(ctx):
        if aligned:
            columns = weight[:, pl.ds(pl.multiple_of(place(k) * block, 128), block)]
        else:
            columns = weight[:, k * block:(k + 1) * block]
        part = jnp.dot(head_out, columns, preferred_element_type=F32)
        low, high = part[:, :half], part[:, half:]
        h_keep[k] = jnp.where(core == 0, low, high)
        h_out[k] = jnp.where(core == 0, high, low)
        copy = remote(h_out.at[k], h_in.at[k], h_send.at[k], h_recv.at[k], twin)
        copy.start()
        h_copies.append(copy)
        if k > 0:
            forward(k - 1)
    forward(ctx - 1)
    if aligned:
        result = h_keep[ctx - 1] + h_in[ctx - 1]
    else:
        result = p_out[me].astype(F32)
    for k in range(ctx - 1):
        remote(p_out.at[k], p_in.at[k], p_send.at[k], p_recv.at[k], partner).wait_recv()
        result = result + p_in[k].astype(F32)
    out_ref[...] = result.astype(BF16)
    for k in range(ctx - 1):
        remote(p_out.at[k], p_in.at[k], p_send.at[k], p_recv.at[k], partner).wait_send()
    for copy in h_copies + z_copies + z_stats + y_copies + [stat_copy]:
        copy.wait_send()
    for which in range(2):
        for part in range(PARTS):
            for origin in range(nz):
                across(which, origin, part, mine[which]).wait_send()
            for step in range(nz - 1):
                @pl.when(has_above & (z - step >= 0))
                def _():
                    upward(which, step, part, mine[which]).wait_send()

                @pl.when(has_below & (z + step < nz))
                def _():
                    downward(which, step, part, mine[which]).wait_send()


def body(ctx, query_nope, query_rope, key_absorb, value_absorb, output_weight, latent_cache, page_owner):
    requests, heads_here, nope = query_nope.shape
    latent = key_absorb.shape[2]
    rope = query_rope.shape[1] // heads_here
    page_count, page, entry = latent_cache.shape
    heads = ctx * heads_here
    cut = latent // 2
    rows = requests * heads_here
    nz = ctx // 2
    half = output_weight.shape[1] // (2 * ctx)
    wanted = -(-page_count // GROUP) + requests - 1
    unroll = min(wanted, 24)
    items = up_to(wanted, unroll)
    table_lanes = up_to(items, 128)
    vmem, dma = pltpu.VMEM, pltpu.SemaphoreType.DMA
    gather_sems = 2 * nz * PARTS
    stat_tail = (2, heads_here, 128)
    operands = [query_nope, query_rope, key_absorb, page_owner.reshape(1, page_count), latent_cache, value_absorb,
                output_weight]
    operands = [pltpu.with_memory_space_constraint(x, pltpu.HBM) for x in operands]
    return pl.pallas_call(
        functools.partial(kernel, ctx, unroll, (nope + rope) ** (-0.5)),
        out_shape=jax.ShapeDtypeStruct((requests, half), BF16),
        in_specs=[pl.BlockSpec(memory_space=pltpu.HBM)] * 7,
        out_specs=pl.BlockSpec(memory_space=pltpu.VMEM),
        scratch_shapes=[
            vmem(query_nope.shape, BF16),
            vmem(query_rope.shape, BF16),
            vmem(key_absorb.shape, BF16),
            vmem(value_absorb.shape, BF16),
            vmem(output_weight.shape, BF16),
            vmem(latent_cache.shape, BF16),
            dma((8,)),
            vmem(query_nope.shape, F32),
            vmem((requests, heads_here, cut + rope), F32),
            vmem((requests, heads_here, latent - cut), F32),
            vmem((rows, cut + rope), BF16),
            vmem((rows, latent - cut), BF16),
            vmem((ctx, rows, cut + rope), BF16),
            vmem((ctx, rows, latent - cut), BF16),
            dma((gather_sems,)), dma((gather_sems,)), dma((gather_sems,)),
            dma((gather_sems,)), dma((gather_sems,)), dma((gather_sems,)),
            vmem((1, page_count), I32),
            vmem((up_to(GROUP + 4, 8), table_lanes), I32),
            pltpu.SMEM((up_to(GROUP + 4, 8), table_lanes), I32),
            vmem((items, GROUP * page), F32),
            vmem((requests, heads, cut + rope), BF16),
            vmem((requests, heads, latent - cut), BF16),
            vmem((items, heads, GROUP * page), F32),
            vmem((items, heads, 128), F32),
            vmem((requests, heads, 128), F32),
            vmem((items, heads, latent), F32),
            vmem((2, nz, rows, latent), BF16),
            vmem((2, nz) + stat_tail, F32),
            vmem((nz, rows, latent), BF16),
            vmem((nz,) + stat_tail, F32),
            vmem((nz - 1, rows, latent), BF16),
            vmem((nz - 1,) + stat_tail, F32),
            vmem((nz - 1, rows, latent), BF16),
            vmem((nz - 1,) + stat_tail, F32),
            vmem((requests, heads_here, latent), F32),
            vmem((ctx, requests, half), F32),
            vmem((ctx, requests, half), F32),
            vmem((ctx, requests, half), F32),
            vmem((ctx, requests, half), BF16),
            vmem((ctx - 1, requests, half), BF16),
            dma((nz * PARTS,)), dma((nz * PARTS,)), dma, dma,
            dma(((nz - 1) * PARTS,)), dma(((nz - 1) * PARTS,)), dma((nz - 1,)), dma((nz - 1,)),
            dma((ctx,)), dma((ctx,)), dma((ctx - 1,)), dma((ctx - 1,)),
        ],
        compiler_params=pltpu.CompilerParams(collective_id=0, has_side_effects=True, vmem_limit_bytes=62 << 20),
    )(*operands)


def solution(mesh):
    return jax.shard_map(
        functools.partial(body, mesh.shape["ctx"]),
        mesh=mesh,
        in_specs=(
            P("groups", ("ctx", "head"), None),
            P("groups", ("ctx", "head")),
            P(("ctx", "head"), None, None),
            P(("ctx", "head"), None, None),
            P(("ctx", "head"), None),
            P(("groups", "ctx"), None, None),
            P(("groups", "ctx")),
        ),
        out_specs=P("groups", ("ctx", "head")),
        check_vma=False,
    )
```

time: 64.7 us -> 58.2 us (0.90)
  Pallas kernels: 63.9 us -> 56.6 us
  local copies, waits for them, and re-layouts: 0.61 us -> 1.32 us
    pallas_call x3 -> x1, Pallas kernels: 63.9 us -> 56.6 us  [body(): pl.pallas_call(functools.partial(kernel, ctx, unroll, (nope + rope) ** (-...]
    unnamed x3 -> x1, local copies, waits for them, and re-layouts: 0.61 us -> 1.32 us
where the time goes in v1:
time: 58.2 us; the launch traced here: 57.9 us
  Pallas kernels  56.6 us (97%)
  local copies, waits for them, and re-layouts  1.32 us (2%)
    pallas_call x1, Pallas kernels, body(): pl.pallas_call(functools.partial(kernel, ctx, unroll, (nope + rope) ** (-...  56.6 us
    unnamed x1, local copies, waits for them, and re-layouts  1.32 us

profile of v1, /device:TPU:0, one launch (start us, length us, event | category | flops | bytes accessed | tf_op | source)
XLA Modules:
  0.0 57.9 jit_solution(5813217996324659805)
XLA Ops:
  0.0 56.6 %shard_map.73 = bf16[16,448]{1,0:T(8,128)(2,1)} custom-call(bf16[16,8,128]{2,1,0:T(8,128)(2,1)} %nope_hbm.1, bf16[16,512]{1,0:T(8,128)(2,1)} %rope_hbm.1, bf16[8,128,512]{2,1,0:T(8,128)(2,1)} %key_hbm.1, s32[1,224]{1,0:T(1,128)} %bitcast.1, bf16[224,64,576]{2,1,0:T(8,128)(2,1)} %cache_hbm.1, bf16[8,512,128]{2,1,0:T(8,128)(2,1)} %value_hbm.1, ...), custom_call_target="tpu_custom_call" | custom-call | tf_op jit(solution)/shard_map/pallas_call | solution.py:450
  56.6 1.3 %copy.9 = bf16[16,448]{1,0:T(8,128)(2,1)} copy(bf16[16,448]{1,0:T(8,128)(2,1)} %shard_map.73) | data formatting | bytes 28672

commit v2 on v1

--- a/solution.py
+++ b/solution.py
@@ -9,6 +9,7 @@
 
 PARTS = 2
 GROUP = 4
+LAG = 4
 F32 = jnp.float32
 BF16 = jnp.bfloat16
 I32 = jnp.int32
@@ -27,6 +28,10 @@
 
 def up_to(n, step):
     return -(-n // step) * step
+
+
+def spaced(columns):
+    return (columns // 128 | 1) * 128 if columns % 128 == 0 else columns
 
 
 def column(row):
@@ -86,9 +91,9 @@
 
 
 def kernel(ctx, unroll, score_scale, nope_hbm, rope_hbm, key_hbm, owner_hbm, cache_hbm, value_hbm, weight_hbm, out_ref,
-           nope_ref, rope_ref, key_ref, value_ref, weight, pages, in_sems, wide, rows_a, rows_b, mine_a, mine_b,
-           all_a, all_b, y_send, y_recv, up_send, up_recv, down_send, down_recv,
-           owner_ref, table, tab, bias, query_a, query_b, scores, marks, top_full, acc,
+           nope_ref, rope_ref, key_ref, value_ref, weight, pages, in_sems, wide, rows_a, rows_b, rows_c, mine_a, mine_b, mine_c,
+           all_a, all_b, all_c, y_send, y_recv, up_send, up_recv, down_send, down_recv,
+           owner_ref, table, tab, bias, query_a, query_b, query_c, scores, marks, top_full, acc,
            sums, stats, y_sum, y_stat, c_sum, c_stat, z_sum, z_stat, attended,
            h_keep, h_out, h_in, p_out, p_in,
            ys_send, ys_recv, yt_send, yt_recv, zs_send, zs_recv, zt_send, zt_recv,
@@ -113,7 +118,7 @@
     first_loads = [load(0, nope_hbm, nope_ref), load(1, rope_hbm, rope_ref), load(2, key_hbm, key_ref)]
     owner_load = load(3, owner_hbm, owner_ref)
     cache_load, value_load, weight_load = (
-        load(4, cache_hbm, pages), load(5, value_hbm, value_ref), load(6, weight_hbm, weight))
+        load(4, cache_hbm, pages), load(5, value_hbm, value_ref), load(6, weight_hbm, weight.at[:, :weight_hbm.shape[1]]))
     table_load = load(7, table, tab)
     for copy in first_loads:
         copy.start()
@@ -129,7 +134,7 @@
     cache_load.start()
     wide[...] = nope_ref[...].astype(F32)
     depth = mine_a.shape[0] // PARTS
-    gathered = (all_a, all_b)
+    gathered = (all_a, all_b, all_c)
 
     def lines(part):
         return slice(part * depth, (part + 1) * depth)
@@ -156,9 +161,9 @@
         slot = block_of(which, row, part)
         return remote(slot, slot, done, done, partner)
 
-    mine = (mine_a, mine_b)
-
-    def send_own(which):
+    mine = (mine_a, mine_b, mine_c)
+
+    def send_along(which):
         for part in range(PARTS):
             @pl.when(has_above)
             def _():
@@ -168,23 +173,28 @@
             def _():
                 downward(which, 0, part, mine[which]).start()
 
+    def send_across(which):
+        for part in range(PARTS):
             across(which, z, part, mine[which]).start()
 
     for h in range(heads_here):
-        flat = wide[:, h, :].astype(BF16)
-        rows_a[:, h, :cut] = jnp.dot(flat, key_ref[h, :, :cut], preferred_element_type=F32)
-        rows_a[:, h, cut:] = rope_ref[:, h * rope:(h + 1) * rope].astype(F32)
-    value = rows_a[...].reshape(requests * heads_here, cut + rope).astype(BF16)
-    mine_a[...] = value
-    all_a[me] = value
+        rows_c[:, h, :] = rope_ref[:, h * rope:(h + 1) * rope].astype(F32)
+        rows_a[:, h, :] = jnp.dot(wide[:, h, :].astype(BF16), key_ref[h, :, :cut], preferred_element_type=F32)
+    for which, rows in ((2, rows_c), (0, rows_a)):
+        value = rows[...].reshape(requests * heads_here, rows.shape[2]).astype(BF16)
+        mine[which][...] = value
+        gathered[which][me] = value
     pl.semaphore_wait(barrier, ctx)
-    send_own(0)
+    for which in (2, 0):
+        send_along(which)
+        send_across(which)
     for h in range(heads_here):
         rows_b[:, h, :] = jnp.dot(wide[:, h, :].astype(BF16), key_ref[h, :, cut:], preferred_element_type=F32)
     value = rows_b[...].reshape(requests * heads_here, latent - cut).astype(BF16)
     mine_b[...] = value
     all_b[me] = value
-    send_own(1)
+    send_along(1)
+    send_across(1)
     value_load.start()
     weight_load.start()
 
@@ -213,10 +223,10 @@
                 across(which, z + 1 + step, part).start()
 
     for step in range(nz - 1):
+        pass_on(2, step)
         pass_on(0, step)
-        if step >= 1:
+        if 1 <= step < nz - 2:
             pass_on(1, step - 1)
-    pass_on(1, nz - 2)
 
     def settle(which, query):
         for origin in range(nz):
@@ -226,22 +236,35 @@
             lots = [gathered[which][c, r * heads_here:(r + 1) * heads_here, :].astype(F32) for c in range(ctx)]
             query[r] = jnp.concatenate(lots, axis=0).astype(BF16)
 
-    settle(0, query_a)
     table_load.wait()
     cache_load.wait()
 
     def entries(i, columns):
         return jnp.concatenate([pages[tab[1 + j, i], :, columns] for j in range(GROUP)], axis=0)
+
+    def rope_scores(s, carry):
+        for u in range(unroll):
+            i = s * unroll + u
+            scores[i] = dot_nt(query_c[tab[0, i]], entries(i, slice(latent, latent + rope)))
+        return carry
 
     def first_scores(s, carry):
         for u in range(unroll):
             i = s * unroll + u
-            asked = query_a.at[tab[0, i]]
-            scores[i] = (dot_nt(asked[:, :cut], entries(i, slice(0, cut)))
-                         + dot_nt(asked[:, cut:], entries(i, slice(latent, latent + rope))))
+            scores[i] = scores[i] + dot_nt(query_a[tab[0, i]], entries(i, slice(0, cut)))
         return carry
 
-    lax.fori_loop(0, items // unroll, first_scores, 0)
+    settle(2, query_c)
+    slices = items // unroll
+    left = [step for step in range(nz - 1) if step == nz - 2 or step == nz - 3]
+    for n in range(slices):
+        lax.fori_loop(n, n + 1, rope_scores, 0)
+        if n < len(left) and n < slices - 1:
+            pass_on(1, left[n])
+    for step in left[slices - 1:]:
+        pass_on(1, step)
+    settle(0, query_a)
+    lax.fori_loop(0, slices, first_scores, 0)
     settle(1, query_b)
 
     def last_scores(s, top):
@@ -295,11 +318,14 @@
         lots = [acc[tab[GROUP + 2, r], rows, :] for r in range(requests)]
         sums[c % 2, c // 2] = jnp.concatenate(lots, axis=0).astype(BF16)
 
+    def opposite(k):
+        return z ^ (nz - 1 - k) if nz & (nz - 1) == 0 else (z + 1 + k) % nz
+
     stat_copy = remote(stats.at[1 - y], y_stat, yt_send, yt_recv, partner)
     stat_copy.start()
     y_copies = []
     for k in range(nz):
-        target = (z + 1 + k) % nz
+        target = opposite(k)
         for part in range(PARTS):
             i = k * PARTS + part
             copy = remote(sums.at[1 - y, target, lines(part)], y_sum.at[k, lines(part)],
@@ -313,7 +339,7 @@
 
     z_copies, z_stats = [], []
     for k in range(nz):
-        target = (z + 1 + k) % nz
+        target = opposite(k)
         top_a, norm_a = stats[y, target, 0], stats[y, target, 1]
         top_b, norm_b = y_stat[target, 0], y_stat[target, 1]
         top = jnp.maximum(top_a, top_b)
@@ -368,7 +394,9 @@
     h_copies, p_copies = [], []
 
     def place(k):
-        return (me + 1 + k) % ctx if aligned else k
+        if not aligned:
+            return k
+        return me ^ (ctx - 1 - k) if ctx & (ctx - 1) == 0 else (me + 1 + k) % ctx
 
     def forward(k):
         target = place(k)
@@ -398,9 +426,10 @@
         copy = remote(h_out.at[k], h_in.at[k], h_send.at[k], h_recv.at[k], twin)
         copy.start()
         h_copies.append(copy)
-        if k > 0:
-            forward(k - 1)
-    forward(ctx - 1)
+        if k >= LAG:
+            forward(k - LAG)
+    for k in range(max(ctx - LAG, 0), ctx):
+        forward(k)
     if aligned:
         result = h_keep[ctx - 1] + h_in[ctx - 1]
     else:
@@ -413,7 +442,7 @@
         remote(p_out.at[k], p_in.at[k], p_send.at[k], p_recv.at[k], partner).wait_send()
     for copy in h_copies + z_copies + z_stats + y_copies + [stat_copy]:
         copy.wait_send()
-    for which in range(2):
+    for which in range(3):
         for part in range(PARTS):
             for origin in range(nz):
                 across(which, origin, part, mine[which]).wait_send()
@@ -442,7 +471,7 @@
     items = up_to(wanted, unroll)
     table_lanes = up_to(items, 128)
     vmem, dma = pltpu.VMEM, pltpu.SemaphoreType.DMA
-    gather_sems = 2 * nz * PARTS
+    gather_sems = 3 * nz * PARTS
     stat_tail = (2, heads_here, 128)
     operands = [query_nope, query_rope, key_absorb, page_owner.reshape(1, page_count), latent_cache, value_absorb,
                 output_weight]
@@ -457,24 +486,28 @@
             vmem(query_rope.shape, BF16),
             vmem(key_absorb.shape, BF16),
             vmem(value_absorb.shape, BF16),
-            vmem(output_weight.shape, BF16),
+            vmem((output_weight.shape[0], spaced(output_weight.shape[1])), BF16),
             vmem(latent_cache.shape, BF16),
             dma((8,)),
             vmem(query_nope.shape, F32),
-            vmem((requests, heads_here, cut + rope), F32),
+            vmem((requests, heads_here, cut), F32),
             vmem((requests, heads_here, latent - cut), F32),
-            vmem((rows, cut + rope), BF16),
+            vmem((requests, heads_here, rope), F32),
+            vmem((rows, cut), BF16),
             vmem((rows, latent - cut), BF16),
-            vmem((ctx, rows, cut + rope), BF16),
+            vmem((rows, rope), BF16),
+            vmem((ctx, rows, cut), BF16),
             vmem((ctx, rows, latent - cut), BF16),
+            vmem((ctx, rows, rope), BF16),
             dma((gather_sems,)), dma((gather_sems,)), dma((gather_sems,)),
             dma((gather_sems,)), dma((gather_sems,)), dma((gather_sems,)),
             vmem((1, page_count), I32),
             vmem((up_to(GROUP + 4, 8), table_lanes), I32),
             pltpu.SMEM((up_to(GROUP + 4, 8), table_lanes), I32),
             vmem((items, GROUP * page), F32),
-            vmem((requests, heads, cut + rope), BF16),
+            vmem((requests, heads, cut), BF16),
             vmem((requests, heads, latent - cut), BF16),
+            vmem((requests, heads, rope), BF16),
             vmem((items, heads, GROUP * page), F32),
             vmem((items, heads, 128), F32),
             vmem((requests, heads, 128), F32),

time: 58.2 us -> 57.2 us (0.983)
  Pallas kernels: 56.6 us -> 55.7 us
    pallas_call x1, Pallas kernels: 56.6 us -> 55.7 us  [body(): pl.pallas_call(functools.partial(kernel, ctx, unroll, (nope + rope) ** (-...]
where the time goes in v2:
time: 57.2 us; the launch traced here: 57 us
  Pallas kernels  55.7 us (97%)
  local copies, waits for them, and re-layouts  1.32 us (2%)
    pallas_call x1, Pallas kernels, body(): pl.pallas_call(functools.partial(kernel, ctx, unroll, (nope + rope) ** (-...  55.7 us
    unnamed x1, local copies, waits for them, and re-layouts  1.32 us

profile of v2, /device:TPU:0, one launch (start us, length us, event | category | flops | bytes accessed | tf_op | source)
XLA Modules:
  0.0 57.0 jit_solution(1178064922567209738)
XLA Ops:
  0.0 55.7 %shard_map.73 = bf16[16,448]{1,0:T(8,128)(2,1)} custom-call(bf16[16,8,128]{2,1,0:T(8,128)(2,1)} %nope_hbm.1, bf16[16,512]{1,0:T(8,128)(2,1)} %rope_hbm.1, bf16[8,128,512]{2,1,0:T(8,128)(2,1)} %key_hbm.1, s32[1,224]{1,0:T(1,128)} %bitcast.1, bf16[224,64,576]{2,1,0:T(8,128)(2,1)} %cache_hbm.1, bf16[8,512,128]{2,1,0:T(8,128)(2,1)} %value_hbm.1, ...), custom_call_target="tpu_custom_call" | custom-call | tf_op jit(solution)/shard_map/pallas_call | solution.py:479
  55.7 1.3 %copy.9 = bf16[16,448]{1,0:T(8,128)(2,1)} copy(bf16[16,448]{1,0:T(8,128)(2,1)} %shard_map.73) | data formatting | bytes 28672

commit v3 on v2

--- a/solution.py
+++ b/solution.py
@@ -8,8 +8,10 @@
 from jax.sharding import PartitionSpec as P
 
 PARTS = 2
+FIRST, SECOND, ROTARY = range(3)
 GROUP = 4
-LAG = 4
+BATCH = 3
+UNROLLED = 2
 F32 = jnp.float32
 BF16 = jnp.bfloat16
 I32 = jnp.int32
@@ -59,10 +61,11 @@
     here = rank == lanes
     order = jnp.sum(jnp.where(here, slot, 0), axis=0, keepdims=True)
     sorted_owner = jnp.sum(jnp.where(here, owner_c, 0), axis=0, keepdims=True)
-    before = jnp.sum(jnp.where(rank + 1 == lanes, owner_c, 0), axis=0, keepdims=True)
-    opens = (lax.rem(lane, jnp.full(lane.shape, group, I32)) == 0) | (sorted_owner != before)
+    sorted_c = column(sorted_owner)
+    ahead = jnp.sum(jnp.where(sorted_c < sorted_owner, 1, 0), axis=0, keepdims=True)
+    opens = lax.rem(lane - ahead, jnp.full(lane.shape, group, I32)) == 0
     start = column(jnp.where(opens & (sorted_owner < requests), 1, 0))
-    order_c, sorted_c = column(order), column(sorted_owner)
+    order_c = jnp.minimum(column(order), count - 1)
     item = column(jnp.sum(jnp.where(places <= lanes, start, 0), axis=0, keepdims=True) - 1)
     place = lax.broadcasted_iota(I32, (width, lanes_out), 0)
     mine = (item == lax.broadcasted_iota(I32, (width, lanes_out), 1)) & (start > 0)
@@ -71,14 +74,13 @@
         return jnp.sum(jnp.where(mine, value, 0), axis=0, keepdims=True)
 
     first, who, real = pick(slot), pick(sorted_c), pick(start)
-    first = first - lax.rem(first, jnp.full(first.shape, group, I32))
     tag = jnp.where(real > 0, who, -1)
     tag_c = column(tag)
     table[0:1, :] = who
     for j in range(group):
         chosen = place == first + j
         table[1 + j:2 + j, :] = jnp.sum(jnp.where(chosen, order_c, 0), axis=0, keepdims=True)
-        theirs = column(jnp.sum(jnp.where(chosen, sorted_c, 0), axis=0, keepdims=True))
+        theirs = column(jnp.sum(jnp.where(chosen, sorted_c + 1, 0), axis=0, keepdims=True) - 1)
         fits = jnp.where(theirs[:items] == tag_c[:items], 0.0, LOW)
         bias[:, j * page:(j + 1) * page] = jnp.broadcast_to(fits, (items, page))
     index = lax.broadcasted_iota(I32, (1, lanes_out), 1)
@@ -91,13 +93,13 @@
 
 
 def kernel(ctx, unroll, score_scale, nope_hbm, rope_hbm, key_hbm, owner_hbm, cache_hbm, value_hbm, weight_hbm, out_ref,
-           nope_ref, rope_ref, key_ref, value_ref, weight, pages, in_sems, wide, rows_a, rows_b, rows_c, mine_a, mine_b, mine_c,
+           nope_ref, rope_ref, key_ref, value_ref, weight, pages, in_sems, wide, rows_a, rows_b, rows_c, mine_a, mine_b,
            all_a, all_b, all_c, y_send, y_recv, up_send, up_recv, down_send, down_recv,
            owner_ref, table, tab, bias, query_a, query_b, query_c, scores, marks, top_full, acc,
            sums, stats, y_sum, y_stat, c_sum, c_stat, z_sum, z_stat, attended,
-           h_keep, h_out, h_in, p_out, p_in,
+           p_out, p_in,
            ys_send, ys_recv, yt_send, yt_recv, zs_send, zs_recv, zt_send, zt_recv,
-           h_send, h_recv, p_send, p_recv):
+           p_send, p_recv):
     requests, heads_here, _ = nope_ref.shape
     latent = key_ref.shape[2]
     cut = query_b.shape[2]
@@ -127,6 +129,8 @@
     barrier = pltpu.get_barrier_semaphore()
     for k in range(1, ctx):
         pl.semaphore_signal(barrier, inc=1, device_id={"ctx": (me + k) % ctx}, device_id_type=pl.DeviceIdType.MESH)
+        pl.semaphore_signal(barrier, inc=1, device_id={"ctx": (me + k) % ctx, "head": 1 - core},
+                            device_id_type=pl.DeviceIdType.MESH)
     pl.semaphore_signal(barrier, inc=1, device_id=twin, device_id_type=pl.DeviceIdType.MESH)
 
     for copy in first_loads:
@@ -139,32 +143,38 @@
     def lines(part):
         return slice(part * depth, (part + 1) * depth)
 
+    def parts(which):
+        return range(1 if which == ROTARY else PARTS)
+
+    def piece(which, part):
+        return slice(0, requests) if which == ROTARY else lines(part)
+
     def block_of(which, row, part):
-        return gathered[which].at[row, lines(part)]
+        return gathered[which].at[row, piece(which, part)]
 
     def sem(which, step, part):
         return (which * nz + step) * PARTS + part
 
     def across(which, origin, part, src=None):
         slot, i = block_of(which, origin * 2 + y, part), sem(which, origin, part)
-        return remote(slot if src is None else src.at[lines(part)], slot, y_send.at[i], y_recv.at[i], partner)
+        return remote(slot if src is None else src.at[piece(which, part)], slot, y_send.at[i], y_recv.at[i], partner)
 
     def upward(which, step, part, src=None):
         slot, i = block_of(which, me - 2 * step, part), sem(which, step, part)
-        return remote(slot if src is None else src.at[lines(part)], slot, up_send.at[i], up_recv.at[i], above)
+        return remote(slot if src is None else src.at[piece(which, part)], slot, up_send.at[i], up_recv.at[i], above)
 
     def downward(which, step, part, src=None):
         slot, i = block_of(which, me + 2 * step, part), sem(which, step, part)
-        return remote(slot if src is None else src.at[lines(part)], slot, down_send.at[i], down_recv.at[i], below)
+        return remote(slot if src is None else src.at[piece(which, part)], slot, down_send.at[i], down_recv.at[i], below)
 
     def arrival(which, row, part, done):
         slot = block_of(which, row, part)
         return remote(slot, slot, done, done, partner)
 
-    mine = (mine_a, mine_b, mine_c)
+    mine = (mine_a, mine_b, rope_ref)
 
     def send_along(which):
-        for part in range(PARTS):
+        for part in parts(which):
             @pl.when(has_above)
             def _():
                 upward(which, 0, part, mine[which]).start()
@@ -174,17 +184,16 @@
                 downward(which, 0, part, mine[which]).start()
 
     def send_across(which):
-        for part in range(PARTS):
+        for part in parts(which):
             across(which, z, part, mine[which]).start()
 
+    all_c[me] = rope_ref[...]
     for h in range(heads_here):
-        rows_c[:, h, :] = rope_ref[:, h * rope:(h + 1) * rope].astype(F32)
         rows_a[:, h, :] = jnp.dot(wide[:, h, :].astype(BF16), key_ref[h, :, :cut], preferred_element_type=F32)
-    for which, rows in ((2, rows_c), (0, rows_a)):
-        value = rows[...].reshape(requests * heads_here, rows.shape[2]).astype(BF16)
-        mine[which][...] = value
-        gathered[which][me] = value
-    pl.semaphore_wait(barrier, ctx)
+    value = rows_a[...].reshape(requests * heads_here, cut).astype(BF16)
+    mine_a[...] = value
+    all_a[me] = value
+    pl.semaphore_wait(barrier, 2 * ctx - 1)
     for which in (2, 0):
         send_along(which)
         send_across(which)
@@ -203,7 +212,7 @@
     table_load.start()
 
     def pass_on(which, step):
-        for part in range(PARTS):
+        for part in parts(which):
             @pl.when(z - 1 - step >= 0)
             def _():
                 arrival(which, me - 2 * (step + 1), part, up_recv.at[sem(which, step, part)]).wait_recv()
@@ -230,8 +239,14 @@
 
     def settle(which, query):
         for origin in range(nz):
-            for part in range(PARTS):
+            for part in parts(which):
                 arrival(which, origin * 2 + 1 - y, part, y_recv.at[sem(which, origin, part)]).wait_recv()
+        if which == ROTARY:
+            for c in range(ctx):
+                for h in range(heads_here):
+                    rows_c[:, c * heads_here + h, :] = all_c[c, :, h * rope:(h + 1) * rope].astype(F32)
+            query[...] = rows_c[...].astype(BF16)
+            return
         for r in range(requests):
             lots = [gathered[which][c, r * heads_here:(r + 1) * heads_here, :].astype(F32) for c in range(ctx)]
             query[r] = jnp.concatenate(lots, axis=0).astype(BF16)
@@ -391,59 +406,58 @@
     weight_load.wait()
 
     aligned = block % 128 == 0
-    h_copies, p_copies = [], []
+    powers = ctx & (ctx - 1) == 0
+    own = ctx - 1 if aligned else 0
 
     def place(k):
         if not aligned:
             return k
-        return me ^ (ctx - 1 - k) if ctx & (ctx - 1) == 0 else (me + 1 + k) % ctx
-
-    def forward(k):
+        return me ^ (ctx - 1 - k) if powers else (me + 1 + k) % ctx
+
+    def send_out(k, side):
         target = place(k)
-        h_copies[k].wait_recv()
-        merged = h_keep[k] + h_in[k]
-        p_out[k] = merged.astype(BF16)
-        if aligned:
-            if k < ctx - 1:
-                copy = remote(p_out.at[k], p_in.at[k], p_send.at[k], p_recv.at[k], {"ctx": target})
-                copy.start()
-                p_copies.append(copy)
-        else:
-            @pl.when(target != me)
-            def _():
-                slot = (target - me + ctx - 1) % ctx
-                remote(p_out.at[k], p_in.at[slot], p_send.at[slot], p_recv.at[slot], {"ctx": target}).start()
-
+        slot = (k if aligned else (target - me + ctx) % ctx) * 2 + core
+        return remote(p_out.at[k * 2 + side], p_in.at[slot], p_send.at[k * 2 + side], p_recv.at[slot],
+                      {"ctx": target, "head": side})
+
+    def each_out(k, act):
+        for side in range(2):
+            if aligned and k != own:
+                act(send_out(k, side))
+            else:
+                @pl.when((place(k) != me) | (core != side))
+                def _():
+                    act(send_out(k, side))
+
+    for base in range(0, ctx, BATCH):
+        batch = range(base, min(base + BATCH, ctx))
+        for k in batch:
+            if aligned:
+                columns = weight[:, pl.ds(pl.multiple_of(place(k) * block, 128), block)]
+            else:
+                columns = weight[:, k * block:(k + 1) * block]
+            part = jnp.dot(head_out, columns, preferred_element_type=F32).astype(BF16)
+            p_out[k * 2] = part[:, :half]
+            p_out[k * 2 + 1] = part[:, half:]
+        for k in batch:
+            each_out(k, lambda copy: copy.start())
+    result = p_out[(own if aligned else me) * 2 + core].astype(F32)
     for k in range(ctx):
-        if aligned:
-            columns = weight[:, pl.ds(pl.multiple_of(place(k) * block, 128), block)]
-        else:
-            columns = weight[:, k * block:(k + 1) * block]
-        part = jnp.dot(head_out, columns, preferred_element_type=F32)
-        low, high = part[:, :half], part[:, half:]
-        h_keep[k] = jnp.where(core == 0, low, high)
-        h_out[k] = jnp.where(core == 0, high, low)
-        copy = remote(h_out.at[k], h_in.at[k], h_send.at[k], h_recv.at[k], twin)
-        copy.start()
-        h_copies.append(copy)
-        if k >= LAG:
-            forward(k - LAG)
-    for k in range(max(ctx - LAG, 0), ctx):
-        forward(k)
-    if aligned:
-        result = h_keep[ctx - 1] + h_in[ctx - 1]
-    else:
-        result = p_out[me].astype(F32)
-    for k in range(ctx - 1):
-        remote(p_out.at[k], p_in.at[k], p_send.at[k], p_recv.at[k], partner).wait_recv()
-        result = result + p_in[k].astype(F32)
+        for side in range(2):
+            slot = k * 2 + side
+            if k != own:
+                remote(p_in.at[slot], p_in.at[slot], p_recv.at[slot], p_recv.at[slot], twin).wait_recv()
+                result = result + p_in[slot].astype(F32)
+    far = own * 2 + 1 - core
+    remote(p_in.at[far], p_in.at[far], p_recv.at[far], p_recv.at[far], twin).wait_recv()
+    result = result + p_in[far].astype(F32)
     out_ref[...] = result.astype(BF16)
-    for k in range(ctx - 1):
-        remote(p_out.at[k], p_in.at[k], p_send.at[k], p_recv.at[k], partner).wait_send()
-    for copy in h_copies + z_copies + z_stats + y_copies + [stat_copy]:
+    for k in range(ctx):
+        each_out(k, lambda copy: copy.wait_send())
+    for copy in z_copies + z_stats + y_copies + [stat_copy]:
         copy.wait_send()
-    for which in range(3):
-        for part in range(PARTS):
+    for which in (FIRST, SECOND, ROTARY):
+        for part in parts(which):
             for origin in range(nz):
                 across(which, origin, part, mine[which]).wait_send()
             for step in range(nz - 1):
@@ -466,8 +480,8 @@
     rows = requests * heads_here
     nz = ctx // 2
     half = output_weight.shape[1] // (2 * ctx)
-    wanted = -(-page_count // GROUP) + requests - 1
-    unroll = min(wanted, 24)
+    wanted = (page_count + (GROUP - 1) * requests) // GROUP
+    unroll = -(-wanted // UNROLLED)
     items = up_to(wanted, unroll)
     table_lanes = up_to(items, 128)
     vmem, dma = pltpu.VMEM, pltpu.SemaphoreType.DMA
@@ -492,13 +506,12 @@
             vmem(query_nope.shape, F32),
             vmem((requests, heads_here, cut), F32),
             vmem((requests, heads_here, latent - cut), F32),
-            vmem((requests, heads_here, rope), F32),
+            vmem((requests, heads, rope), F32),
             vmem((rows, cut), BF16),
             vmem((rows, latent - cut), BF16),
-            vmem((rows, rope), BF16),
             vmem((ctx, rows, cut), BF16),
             vmem((ctx, rows, latent - cut), BF16),
-            vmem((ctx, rows, rope), BF16),
+            vmem((ctx,) + query_rope.shape, BF16),
             dma((gather_sems,)), dma((gather_sems,)), dma((gather_sems,)),
             dma((gather_sems,)), dma((gather_sems,)), dma((gather_sems,)),
             vmem((1, page_count), I32),
@@ -521,14 +534,11 @@
             vmem((nz - 1, rows, latent), BF16),
             vmem((nz - 1,) + stat_tail, F32),
             vmem((requests, heads_here, latent), F32),
-            vmem((ctx, requests, half), F32),
-            vmem((ctx, requests, half), F32),
-            vmem((ctx, requests, half), F32),
-            vmem((ctx, requests, half), BF16),
-            vmem((ctx - 1, requests, half), BF16),
+            vmem((2 * ctx, requests, half), BF16),
+            vmem((2 * ctx, requests, half), BF16),
             dma((nz * PARTS,)), dma((nz * PARTS,)), dma, dma,
             dma(((nz - 1) * PARTS,)), dma(((nz - 1) * PARTS,)), dma((nz - 1,)), dma((nz - 1,)),
-            dma((ctx,)), dma((ctx,)), dma((ctx - 1,)), dma((ctx - 1,)),
+            dma((2 * ctx,)), dma((2 * ctx,)),
         ],
         compiler_params=pltpu.CompilerParams(collective_id=0, has_side_effects=True, vmem_limit_bytes=62 << 20),
     )(*operands)

time: 57.2 us -> 55.4 us (0.969)
  Pallas kernels: 55.7 us -> 53.9 us
    pallas_call x1, Pallas kernels: 55.7 us -> 53.9 us  [body(): pl.pallas_call(functools.partial(kernel, ctx, unroll, (nope + rope) ** (-...]
where the time goes in v3:
time: 55.4 us; the launch traced here: 55.2 us
  Pallas kernels  53.9 us (97%)
  local copies, waits for them, and re-layouts  1.32 us (2%)
    pallas_call x1, Pallas kernels, body(): pl.pallas_call(functools.partial(kernel, ctx, unroll, (nope + rope) ** (-...  53.9 us
    unnamed x1, local copies, waits for them, and re-layouts  1.32 us

profile of v3, /device:TPU:0, one launch (start us, length us, event | category | flops | bytes accessed | tf_op | source)
XLA Modules:
  0.0 55.2 jit_solution(1700251059999251716)
XLA Ops:
  0.0 53.9 %shard_map.73 = bf16[16,448]{1,0:T(8,128)(2,1)} custom-call(bf16[16,8,128]{2,1,0:T(8,128)(2,1)} %nope_hbm.1, bf16[16,512]{1,0:T(8,128)(2,1)} %rope_hbm.1, bf16[8,128,512]{2,1,0:T(8,128)(2,1)} %key_hbm.1, s32[1,224]{1,0:T(1,128)} %bitcast.1, bf16[224,64,576]{2,1,0:T(8,128)(2,1)} %cache_hbm.1, bf16[8,512,128]{2,1,0:T(8,128)(2,1)} %value_hbm.1, ...), custom_call_target="tpu_custom_call" | custom-call | tf_op jit(solution)/shard_map/pallas_call | solution.py:493
  53.9 1.3 %copy.9 = bf16[16,448]{1,0:T(8,128)(2,1)} copy(bf16[16,448]{1,0:T(8,128)(2,1)} %shard_map.73) | data formatting | bytes 28672

commit v4 on v3

--- a/solution.py
+++ b/solution.py
@@ -8,6 +8,7 @@
 from jax.sharding import PartitionSpec as P
 
 PARTS = 2
+CUTS = 4
 FIRST, SECOND, ROTARY = range(3)
 GROUP = 4
 BATCH = 3
@@ -117,7 +118,9 @@
     def load(i, src, dst):
         return pltpu.make_async_copy(src, dst, in_sems.at[i])
 
-    first_loads = [load(0, nope_hbm, nope_ref), load(1, rope_hbm, rope_ref), load(2, key_hbm, key_ref)]
+    key_loads = [load(2 + 6 * i, key_hbm.at[:, :, columns], key_ref.at[:, :, columns])
+                 for i, columns in enumerate((slice(0, cut), slice(cut, latent)))]
+    first_loads = [load(1, rope_hbm, rope_ref), load(0, nope_hbm, nope_ref)] + key_loads
     owner_load = load(3, owner_hbm, owner_ref)
     cache_load, value_load, weight_load = (
         load(4, cache_hbm, pages), load(5, value_hbm, value_ref), load(6, weight_hbm, weight.at[:, :weight_hbm.shape[1]]))
@@ -133,10 +136,6 @@
                             device_id_type=pl.DeviceIdType.MESH)
     pl.semaphore_signal(barrier, inc=1, device_id=twin, device_id_type=pl.DeviceIdType.MESH)
 
-    for copy in first_loads:
-        copy.wait()
-    cache_load.start()
-    wide[...] = nope_ref[...].astype(F32)
     depth = mine_a.shape[0] // PARTS
     gathered = (all_a, all_b, all_c)
 
@@ -187,16 +186,23 @@
         for part in parts(which):
             across(which, z, part, mine[which]).start()
 
+    first_loads[0].wait()
+    pl.semaphore_wait(barrier, 2 * ctx - 1)
+    send_along(ROTARY)
+    send_across(ROTARY)
     all_c[me] = rope_ref[...]
+    first_loads[1].wait()
+    wide[...] = nope_ref[...].astype(F32)
+    key_loads[0].wait()
     for h in range(heads_here):
         rows_a[:, h, :] = jnp.dot(wide[:, h, :].astype(BF16), key_ref[h, :, :cut], preferred_element_type=F32)
     value = rows_a[...].reshape(requests * heads_here, cut).astype(BF16)
     mine_a[...] = value
     all_a[me] = value
-    pl.semaphore_wait(barrier, 2 * ctx - 1)
-    for which in (2, 0):
-        send_along(which)
-        send_across(which)
+    send_along(FIRST)
+    send_across(FIRST)
+    key_loads[1].wait()
+    cache_load.start()
     for h in range(heads_here):
         rows_b[:, h, :] = jnp.dot(wide[:, h, :].astype(BF16), key_ref[h, :, cut:], preferred_element_type=F32)
     value = rows_b[...].reshape(requests * heads_here, latent - cut).astype(BF16)
@@ -336,14 +342,19 @@
     def opposite(k):
         return z ^ (nz - 1 - k) if nz & (nz - 1) == 0 else (z + 1 + k) % nz
 
+    thin = y_sum.shape[1] // CUTS
+
+    def rows_of(part):
+        return slice(part * thin, (part + 1) * thin)
+
     stat_copy = remote(stats.at[1 - y], y_stat, yt_send, yt_recv, partner)
     stat_copy.start()
     y_copies = []
     for k in range(nz):
         target = opposite(k)
-        for part in range(PARTS):
-            i = k * PARTS + part
-            copy = remote(sums.at[1 - y, target, lines(part)], y_sum.at[k, lines(part)],
+        for part in range(CUTS):
+            i = k * CUTS + part
+            copy = remote(sums.at[1 - y, target, rows_of(part)], y_sum.at[k, rows_of(part)],
                           ys_send.at[i], ys_recv.at[i], partner)
             copy.start()
             y_copies.append(copy)
@@ -369,14 +380,14 @@
             copy.start()
             z_stats.append(copy)
         both = []
-        for part in range(PARTS):
-            i = k * PARTS + part
+        for part in range(CUTS):
+            i = k * CUTS + part
             y_copies[i].wait_recv()
-            both.append(rows_x[lines(part)] * sums[y, target, lines(part)].astype(F32)
-                        + rows_y[lines(part)] * y_sum[k, lines(part)].astype(F32))
+            both.append(rows_x[rows_of(part)] * sums[y, target, rows_of(part)].astype(F32)
+                        + rows_y[rows_of(part)] * y_sum[k, rows_of(part)].astype(F32))
             if k < nz - 1:
-                c_sum[k, lines(part)] = both[part].astype(BF16)
-                copy = remote(c_sum.at[k, lines(part)], z_sum.at[k, lines(part)], zs_send.at[i], zs_recv.at[i], there)
+                c_sum[k, rows_of(part)] = both[part].astype(BF16)
+                copy = remote(c_sum.at[k, rows_of(part)], z_sum.at[k, rows_of(part)], zs_send.at[i], zs_recv.at[i], there)
                 copy.start()
                 z_copies.append(copy)
     both = jnp.concatenate(both, axis=0)
@@ -394,8 +405,8 @@
     safe = jnp.where(all_norm > 0, all_norm, 1.0)
     total = spread(keep / safe) * both
     for k in range(nz - 1):
-        for part in range(PARTS):
-            z_copies[k * PARTS + part].wait_recv()
+        for part in range(CUTS):
+            z_copies[k * CUTS + part].wait_recv()
         total = total + spread(factors[k] / safe) * z_sum[k].astype(F32)
     attended[...] = total.reshape(requests, heads_here, latent)
     outs = []
@@ -492,7 +503,7 @@
     operands = [pltpu.with_memory_space_constraint(x, pltpu.HBM) for x in operands]
     return pl.pallas_call(
         functools.partial(kernel, ctx, unroll, (nope + rope) ** (-0.5)),
-        out_shape=jax.ShapeDtypeStruct((requests, half), BF16),
+        out_shape=pltpu.VMEM((requests, half), BF16),
         in_specs=[pl.BlockSpec(memory_space=pltpu.HBM)] * 7,
         out_specs=pl.BlockSpec(memory_space=pltpu.VMEM),
         scratch_shapes=[
@@ -502,7 +513,7 @@
             vmem(value_absorb.shape, BF16),
             vmem((output_weight.shape[0], spaced(output_weight.shape[1])), BF16),
             vmem(latent_cache.shape, BF16),
-            dma((8,)),
+            dma((9,)),
             vmem(query_nope.shape, F32),
             vmem((requests, heads_here, cut), F32),
             vmem((requests, heads_here, latent - cut), F32),
@@ -536,11 +547,11 @@
             vmem((requests, heads_here, latent), F32),
             vmem((2 * ctx, requests, half), BF16),
             vmem((2 * ctx, requests, half), BF16),
-            dma((nz * PARTS,)), dma((nz * PARTS,)), dma, dma,
-            dma(((nz - 1) * PARTS,)), dma(((nz - 1) * PARTS,)), dma((nz - 1,)), dma((nz - 1,)),
+            dma((nz * CUTS,)), dma((nz * CUTS,)), dma, dma,
+            dma(((nz - 1) * CUTS,)), dma(((nz - 1) * CUTS,)), dma((nz - 1,)), dma((nz - 1,)),
             dma((2 * ctx,)), dma((2 * ctx,)),
         ],
-        compiler_params=pltpu.CompilerParams(collective_id=0, has_side_effects=True, vmem_limit_bytes=62 << 20),
+        compiler_params=pltpu.CompilerParams(collective_id=0, has_side_effects=True, vmem_limit_bytes=58 << 20),
     )(*operands)
 
 

time: 55.4 us -> 54.1 us (0.977)
  local copies, waits for them, and re-layouts: 1.32 us -> 0.61 us
  Pallas kernels: 53.9 us -> 53.3 us
    unnamed x1, local copies, waits for them, and re-layouts: 1.32 us -> 0.61 us
    pallas_call x1, Pallas kernels: 53.9 us -> 53.3 us  [body(): pl.pallas_call(functools.partial(kernel, ctx, unroll, (nope + rope) ** (-...]
where the time goes in v4:
time: 54.1 us; the launch traced here: 53.9 us
  Pallas kernels  53.3 us (99%)
  local copies, waits for them, and re-layouts  0.61 us (1%)
    pallas_call x1, Pallas kernels, body(): pl.pallas_call(functools.partial(kernel, ctx, unroll, (nope + rope) ** (-...  53.3 us

profile of v4, /device:TPU:0, one launch (start us, length us, event | category | flops | bytes accessed | tf_op | source)
XLA Modules:
  0.0 53.9 jit_solution(6975245405336008050)
XLA Ops:
  0.0 53.3 %shard_map.73 = bf16[16,448]{1,0:T(8,128)(2,1)S(1)} custom-call(bf16[16,8,128]{2,1,0:T(8,128)(2,1)} %nope_hbm.1, bf16[16,512]{1,0:T(8,128)(2,1)} %rope_hbm.1, bf16[8,128,512]{2,1,0:T(8,128)(2,1)} %key_hbm.1, s32[1,224]{1,0:T(1,128)} %bitcast.1, bf16[224,64,576]{2,1,0:T(8,128)(2,1)} %cache_hbm.1, bf16[8,512,128]{2,1,0:T(8,128)(2,1)} %value_hbm.1, ...), custom_call_target="tpu_custom_call" | custom-call | tf_op jit(solution)/shard_map/pallas_call | solution.py:504
  53.3 0.6 %copy.9 = bf16[16,448]{1,0:T(8,128)(2,1)} copy(bf16[16,448]{1,0:T(8,128)(2,1)S(1)} %shard_map.73) | data formatting | bytes 28672
